TPU v7x, 512 devices: a whole 4x8x8 slice. The times are simulated.
512 devices in a mesh: dp: 64 (over y, x, core), tensor: 8 (over z).
Axes of the slice: x: 4, y: 8, z: 8, core: 2. Of those that a mesh axis runs over, the one named last changes fastest.
Arguments:
- hidden_act: bfloat16 [32768, 1408], P('dp', 'tensor'), may hold values from -6 to 6
- cotangent: bfloat16 [32768, 2048], P('dp', 'tensor'), may hold values from -4 to 4
- down_table: bfloat16 [1408, 64, 2048], P('tensor', 'dp'), may hold values from -0.15625 to 0.15625
- expert_ids: int32 [128, 4], P('dp'), may hold values from 0 to 31, as said below
- merge_weights: float32 [128, 4], P('dp'), may hold values from 0.1 to 1
- owner_slot: int32 [32], replicated, may hold values from 0 to 63, as said below
Outputs:
- layer_out: bfloat16 [32768, 2048], P('dp', 'tensor')
- grad_hidden: bfloat16 [32768, 1408], P('dp', 'tensor')
- expert_grad: float32 [1408, 64, 2048], P('tensor', 'dp')
Inputs may be any that keep to these rules, and one draw needn't show every extreme that they name: `expert_ids`: each segment lists 4 different experts; the 2 segments of one index of dp list exactly 6 different experts together. `owner_slot`: different experts have different slots; slot 63 always holds an expert.
All inputs are finite; a program needn't handle non-finite values.
Results may differ from a plain program's by a relative error of at most 0.013.
Values may be sent and summed in bfloat16 or wider, within the bound.
A program may use at most 128 MiB of HBM per device.

v0:
```python
import jax
import jax.numpy as jnp
from jax import lax
from jax.sharding import PartitionSpec as P

E = 32
K = 4
POOL = 6


def pool_members(id_rows):
    listed = id_rows.reshape(-1)
    experts = jnp.arange(E, dtype=jnp.int32)
    present = jnp.any(listed[None, :] == experts[:, None], axis=1)
    ranking = jnp.cumsum(present.astype(jnp.int32)) - 1
    places = jnp.arange(POOL, dtype=jnp.int32)
    chosen = present[None, :] & (ranking[None, :] == places[:, None])
    return jnp.sum(jnp.where(chosen, experts[None, :], 0), axis=1)


def merge_coefficients(id_rows, weight_rows, targets):
    matches = id_rows[:, :, None] == targets[None, None, :]
    return jnp.sum(jnp.where(matches, weight_rows[:, :, None], 0.0), axis=1)


def body(hidden_act, cotangent, down_table, expert_ids, merge_weights, owner_slot):
    dp_count = lax.axis_size("dp")
    seg_count = expert_ids.shape[0]
    ff_local, slot_local, width = down_table.shape
    stripe = width // dp_count
    row_count = hidden_act.shape[0]
    seg_len = row_count // seg_count
    every_expert = jnp.arange(E, dtype=jnp.int32)
    all_ids, all_weights = (
        lax.all_gather(expert_ids, "dp", axis=0, tiled=True),
        lax.all_gather(merge_weights, "dp", axis=0, tiled=True),
    )
    ids_by_dev = all_ids.reshape(dp_count, seg_count, K)
    weights_by_dev = all_weights.reshape(dp_count, seg_count, K)
    pools_all = jax.vmap(pool_members)(ids_by_dev)
    my_pool = pools_all[lax.axis_index("dp")]
    my_coef = merge_coefficients(expert_ids, merge_weights, my_pool)
    member_table = (pools_all.T[:, :, None] == every_expert[None, None, :]).astype(jnp.bfloat16)
    stripes = lax.all_to_all(down_table, "dp", split_axis=2, concat_axis=1, tiled=True)
    by_expert = jnp.take(stripes, owner_slot, axis=1)
    outgoing = jnp.take(by_expert, pools_all.T, axis=1).reshape(ff_local, POOL, width)
    panel_set = lax.all_to_all(outgoing, "dp", split_axis=2, concat_axis=2, tiled=True)
    merged = jnp.sum(
        panel_set[:, None, :, :].astype(jnp.float32) * my_coef[None, :, :, None], axis=2
    ).astype(jnp.bfloat16)
    hidden_seg = hidden_act.reshape(seg_count, seg_len, ff_local)
    partial_rows = jnp.einsum(
        "stf,fsd->std", hidden_seg, merged, preferred_element_type=jnp.float32
    ).reshape(row_count, width)
    layer_out = lax.psum_scatter(
        partial_rows.astype(jnp.bfloat16), "tensor", scatter_dimension=1, tiled=True
    )
    full_cot = lax.all_gather(cotangent, "tensor", axis=1, tiled=True)
    cot_seg = full_cot.reshape(seg_count, seg_len, width)
    grad_hidden = (
        jnp.einsum("std,fsd->stf", cot_seg, merged, preferred_element_type=jnp.float32)
        .astype(jnp.bfloat16)
        .reshape(row_count, ff_local)
    )
    seg_grads = jnp.einsum(
        "stf,std->fsd", hidden_seg, cot_seg, preferred_element_type=jnp.float32
    ).astype(jnp.bfloat16)
    returned = lax.all_to_all(seg_grads, "dp", split_axis=2, concat_axis=2, tiled=True).reshape(
        ff_local, seg_count, dp_count, stripe
    )
    pool_coef = jax.vmap(merge_coefficients)(ids_by_dev, weights_by_dev, pools_all)
    coef_view = jnp.transpose(pool_coef, (1, 2, 0))
    group_sums = jnp.sum(
        returned[:, :, None, :, :].astype(jnp.float32) * coef_view[None, :, :, :, None], axis=1
    ).astype(jnp.bfloat16)
    grad_stripes = jnp.einsum(
        "fprd,pre->fed", group_sums, member_table, preferred_element_type=jnp.float32
    )
    slotted = (
        jnp.zeros((ff_local, slot_local * dp_count, stripe), jnp.float32)
        .at[:, owner_slot, :]
        .set(grad_stripes)
    )
    expert_grad = lax.all_to_all(
        slotted.astype(jnp.bfloat16), "dp", split_axis=1, concat_axis=2, tiled=True
    ).astype(slotted.dtype)
    return (layer_out, grad_hidden, expert_grad)


def solution(mesh):
    placed = (
        P("dp", "tensor"),
        P("dp", "tensor"),
        P("tensor", "dp", None),
        P("dp", None),
        P("dp", None),
        P(),
    )
    return jax.shard_map(
        body,
        mesh=mesh,
        in_specs=placed,
        out_specs=(P("dp", "tensor"), P("dp", "tensor"), P("tensor", "dp", None)),
        check_vma=False,
    )
```

profile of v0, /device:TPU:1, one launch (start us, length us, event | category | flops | bytes accessed | tf_op | source)
XLA Modules:
  0.0 478.6 jit_solution(9711148216334973201)
XLA Ops:
  7.2 4.5 copy.81
  11.7 0.5 broadcast.42
  12.2 11.6 %reduce.2 = bf16[2048,176]{1,0:T(8,128)(2,1)S(1)} reduce(bf16[2048,1,176]{2,1,0:T(2,128)(2,1)S(1)} %bitcast.55, bf16[]{:T(256)} %broadcast.42), dimensions={1}, to_apply=%bitcast.44.reduce_sub_computation | reduce | bytes 1441794
  23.9 2.6 reshape.124
  26.5 11.6 %all-to-all-start = ((bf16[64,2,2816]{2,1,0:T(2,128)(2,1)}), bf16[64,2,2816]{2,1,0:T(2,128)(2,1)S(1)}, u32[]{:S(2)}, u32[]{:S(2)}) async-start(bf16[64,2,2816]{2,1,0:T(2,128)(2,1)} %reshape.124), calls=%async_computation | async-start | bytes 1441792 | tf_op jit(solution)/shard_map/all_to_all | solution.py:44
  38.1 50.6 %all-gather = s32[64,2,4]{2,1,0:T(2,128)S(1)} all-gather(s32[1,2,4]{2,1,0:T(2,128)S(1)} %bitcast.65), channel_id=1, replica_groups=mesh['dp'=64,'tensor'=8] {'dp'}, dimensions={0}, use_global_device_ids=true | all-gather | bytes 2080 | tf_op jit(solution)/shard_map/all_gather | solution.py:35
  88.8 0.1 copy.78
  88.9 0.1 copy.79
  89.0 0.2 reduce_window_sum.11
  89.2 0.1 copy.80
  89.3 0.1 reshape.96
  89.4 0.1 broadcast_in_dim.85
  89.5 0.2 broadcast_in_dim.86
  89.8 3.2 reshape.125
  92.9 0.2 copy.95
  93.1 0.6 gather_fusion
  93.7 0.1 select_bitcast_fusion
  93.8 13.3 %gather_fusion.1 = bf16[384,176,32]{1,2,0:T(8,128)(2,1)} fusion(bf16[176,32,32]{0,2,1:T(8,128)(2,1)S(1)} %select_bitcast_fusion, s32[1024]{0:T(1024)S(1)} %pad_clamp_fusion), kind=kCustom, calls=%fused_computation.1 | custom fusion | bytes 8652288 | tf_op jit(solution)/shard_map/jit(_take)/gather | solution.py:46
  107.2 6.2 %broadcast_select_fusion = bf16[176,6,2048]{0,2,1:T(8,128)(2,1)S(1)} fusion(bf16[176,6,2048]{0,2,1:T(8,128)(2,1)} %bitcast.51, pred[6,2048]{1,0:T(8,128)(4,1)S(1)} %broadcast_in_dim.86), kind=kLoop, calls=%fused_computation.7 | loop fusion | flops 2162688 | bytes 8663040 | tf_op jit(solution)/shard_map/jit(_take)/select_n | solution.py:46
  113.4 22.3 %copy.82 = bf16[176,6,2048]{0,1,2:T(8,128)(2,1)} copy(bf16[176,6,2048]{0,2,1:T(8,128)(2,1)S(1)} %broadcast_select_fusion) | data formatting | bytes 8650752 | tf_op jit(solution)/shard_map/jit(_take)/select_n | solution.py:46
  135.7 8.6 %all-to-all-start.1 = ((bf16[176,6,2048]{0,1,2:T(8,128)(2,1)}), bf16[176,6,2048]{0,1,2:T(8,128)(2,1)}, u32[]{:S(2)}, u32[]{:S(2)}) async-start(bf16[176,6,2048]{0,1,2:T(8,128)(2,1)} %copy.82), calls=%async_computation.1 | async-start | bytes 16777216 | tf_op jit(solution)/shard_map/all_to_all | solution.py:47
  144.4 0.7 all-gather.4.cloned.1.call-update
  145.1 53.0 %all-gather.4.cloned.1.call-done = bf16[512,2048]{1,0:T(8,128)(2,1)} async-done(((bf16[512,256]{1,0:T(8,128)(2,1)}), bf16[512,2048]{1,0:T(8,128)(2,1)}) %all-gather.4.cloned.1.call-update) | async-done | bytes 2097168 | tf_op jit(solution)/shard_map/all_gather | solution.py:58
  198.0 2.1 fusion.2
  200.2 3.8 copy.87
  204.0 122.7 %all-to-all-done.1 = bf16[176,6,2048]{0,1,2:T(8,128)(2,1)} async-done(((bf16[176,6,2048]{0,1,2:T(8,128)(2,1)}), bf16[176,6,2048]{0,1,2:T(8,128)(2,1)}, u32[]{:S(2)}, u32[]{:S(2)}) %all-to-all-start.1) | async-done | bytes 4325408 | tf_op jit(solution)/shard_map/all_to_all | solution.py:47
  326.7 10.1 %all-to-all-start.2 = ((bf16[176,2,2048]{0,1,2:T(2,128)(2,1)}), bf16[176,2,2048]{0,1,2:T(2,128)(2,1)S(1)}, u32[]{:S(2)}, u32[]{:S(2)}) async-start(bf16[176,2,2048]{0,1,2:T(2,128)(2,1)} %copy.87), calls=%async_computation.3 | async-start | bytes 4194304 | tf_op jit(solution)/shard_map/all_to_all | solution.py:68
  336.8 0.2 dynamic-slice_reduce_fusion
  337.0 0.1 select_reduce_fusion.2
  337.1 11.3 %copy.83 = bf16[176,6,2048]{2,0,1:T(8,128)(2,1)} copy(bf16[176,6,2048]{0,1,2:T(8,128)(2,1)} %all-to-all-done.1) | data formatting | bytes 8650752 | tf_op jit(solution)/shard_map/all_to_all | solution.py:47
  348.4 6.6 %convert_element_type.68 = f32[176,6,2048]{2,0,1:T(8,128)} convert(bf16[176,6,2048]{2,0,1:T(8,128)(2,1)} %copy.83) | non-fusion elementwise | flops 2162688 | bytes 12976128 | tf_op jit(solution)/shard_map/convert_element_type | solution.py:49
  355.0 4.8 multiply_reduce_fusion.1
  359.8 1.1 copy-done
  360.9 2.1 convolution_convert_fusion
  363.0 53.9 %all-gather.1 = f32[64,2,4]{2,1,0:T(2,128)S(1)} all-gather(f32[1,2,4]{2,1,0:T(2,128)S(1)} %bitcast.66), channel_id=1, replica_groups=mesh['dp'=64,'tensor'=8] {'dp'}, dimensions={0}, use_global_device_ids=true | all-gather | bytes 2080 | tf_op jit(solution)/shard_map/all_gather | solution.py:36
  416.9 0.1 copy.90
  417.0 0.6 bitcast_convert_fusion.1
  417.7 4.2 multiply_reduce_fusion
  421.9 3.7 fusion.3
  425.6 0.6 copy.92
  426.2 0.2 broadcast_in_dim.95
  426.4 1.6 scatter_fusion
  428.0 0.2 convert_element_type.80
  428.2 35.5 %all_to_all.31 = bf16[176,64,32]{0,2,1:T(8,128)(2,1)S(1)} all-to-all(bf16[176,64,32]{0,2,1:T(8,128)(2,1)S(1)} %convert_element_type.80), channel_id=1, replica_groups=mesh['dp'=64,'tensor'=8] {'dp'}, dimensions={1} | all-to-all | bytes 1441792 | tf_op jit(solution)/shard_map/all_to_all | solution.py:84
  463.7 1.5 bitcast_convert_fusion
  465.2 5.1 %copy.93 = f32[176,1,2048]{2,1,0:T(1,128)} copy(f32[176,1,2048]{0,2,1:T(8,128)} %bitcast_convert_fusion) | data formatting | bytes 2883584
  470.2 0.8 fusion.6
  471.1 0.7 copy.97
  (30 shorter events, 0.3 us)
Async XLA Ops:
  23.9 14.3 %copy-start.4 = (s32[2,4]{1,0:T(2,128)S(1)}, s32[2,4]{1,0:T(2,128)}, u32[]{:S(2)}) copy-start(s32[2,4]{1,0:T(2,128)} %param.9) | copy-start | bytes 100
  23.9 65.9 %copy-start.6 = (s32[32]{0:T(128)S(1)}, s32[32]{0:T(128)}, u32[]{:S(2)}) copy-start(s32[32]{0:T(128)} %param.11) | copy-start | bytes 388
  26.5 63.3 %all-to-all-start = ((bf16[64,2,2816]{2,1,0:T(2,128)(2,1)}), bf16[64,2,2816]{2,1,0:T(2,128)(2,1)S(1)}, u32[]{:S(2)}, u32[]{:S(2)}) async-start(bf16[64,2,2816]{2,1,0:T(2,128)(2,1)} %reshape.124), calls=%async_computation | async-start | bytes 1441792 | tf_op jit(solution)/shard_map/all_to_all | solution.py:44
  135.7 62.3 %copy-start.3 = (bf16[512,176]{0,1:T(8,128)(2,1)S(1)}, bf16[512,176]{0,1:T(8,128)(2,1)}, u32[]{:S(2)}) copy-start(bf16[512,176]{0,1:T(8,128)(2,1)} %param.6) | copy-start | bytes 540676
  135.7 191.0 %all-to-all-start.1 = ((bf16[176,6,2048]{0,1,2:T(8,128)(2,1)}), bf16[176,6,2048]{0,1,2:T(8,128)(2,1)}, u32[]{:S(2)}, u32[]{:S(2)}) async-start(bf16[176,6,2048]{0,1,2:T(8,128)(2,1)} %copy.82), calls=%async_computation.1 | async-start | bytes 16777216 | tf_op jit(solution)/shard_map/all_to_all | solution.py:47
  144.3 53.7 %all-gather.4.cloned.1.call-start = ((), (), s32[]{:S(2)}) async-start(), calls=%async_computation.6 | async-start | bytes 2359296 | tf_op jit(solution)/shard_map/all_gather | solution.py:58
  204.0 133.0 %copy-start.5 = (f32[2,4]{1,0:T(2,128)S(1)}, f32[2,4]{1,0:T(2,128)}, u32[]{:S(2)}) copy-start(f32[2,4]{1,0:T(2,128)} %param.10) | copy-start | bytes 100
  326.7 90.3 %all-to-all-start.2 = ((bf16[176,2,2048]{0,1,2:T(2,128)(2,1)}), bf16[176,2,2048]{0,1,2:T(2,128)(2,1)S(1)}, u32[]{:S(2)}, u32[]{:S(2)}) async-start(bf16[176,2,2048]{0,1,2:T(2,128)(2,1)} %copy.87), calls=%async_computation.3 | async-start | bytes 4194304 | tf_op jit(solution)/shard_map/all_to_all | solution.py:68
  336.8 135.0 %reduce-scatter.2.cloned.1.call-start = ((), (), s32[]{:S(2)}) async-start(), calls=%async_computation.5 | async-start | bytes 2359296 | tf_op jit(solution)/shard_map/reduce_scatter | solution.py:55
  359.8 1.1 copy-start
  465.2 5.1 %copy-start.1 = (bf16[176,2,2048]{2,0,1:T(8,128)(2,1)S(1)}, bf16[176,2,2048]{2,0,1:T(8,128)(2,1)}, u32[]{:S(2)}) copy-start(bf16[176,2,2048]{2,0,1:T(8,128)(2,1)} %copy-done) | copy-start | bytes 4325380
  465.2 5.1 %copy-start.2 = (bf16[512,2048]{1,0:T(8,128)(2,1)S(1)}, bf16[512,2048]{1,0:T(8,128)(2,1)}, u32[]{:S(2)}) copy-start(bf16[512,2048]{1,0:T(8,128)(2,1)} %all-gather.4.cloned.1.call-done) | copy-start | bytes 6291460
Sparse Core Ops, SparseCore 0:
  147.2 50.8 all-gather.3
  363.1 45.3 reduce-scatter.1
where the time goes:
time: 480 us; the launch traced here: 479 us
  waiting for transfers between devices  176 us (37%)
  blocking collectives  140 us (29%)
  local copies, waits for them, and re-layouts  72.6 us (15%)
  other arithmetic  36.2 us (8%)
  starting transfers between devices  30.4 us (6%)
  between operations  14.3 us (3%)
  matrix products  8.77 us (2%)
    all_to_all x1, waiting for transfers between devices, body(): lax.all_to_all(outgoing, 'dp', split_axis=2, concat_axis=2, tiled=True)  123 us
    all_gather x1, blocking collectives, body(): lax.all_gather(merge_weights, 'dp', axis=0, tiled=True)  53.9 us
    all_gather x1, waiting for transfers between devices, body(): full_cot = lax.all_gather(cotangent, 'tensor', axis=1, tiled=True)  53 us
    all_gather x1, blocking collectives, body(): lax.all_gather(expert_ids, 'dp', axis=0, tiled=True)  50.6 us
    all_to_all x1, blocking collectives, body(): lax.all_to_all(slotted.astype(jnp.bfloat16), 'dp', split_axis=1, concat_a...  35.5 us
    select_n x1, local copies, waits for them, and re-layouts, body(): jnp.take(by_expert, pools_all.T, axis=1).reshape(ff_local, POOL, width)  22.3 us
    unnamed x20, local copies, waits for them, and re-layouts  17.2 us
    gather x1, local copies, waits for them, and re-layouts, body(): jnp.take(by_expert, pools_all.T, axis=1).reshape(ff_local, POOL, width)  13.3 us
  transfers between devices with their start and end apart: 5, of which 2 were waited for; matrix products, arithmetic and copies ran while one was open for 11% of the time, Pallas kernels for 0%

commit v1 on v0

--- a/solution.py
+++ b/solution.py
@@ -2,6 +2,7 @@
 import jax.numpy as jnp
 from jax import lax
 from jax.sharding import PartitionSpec as P
+from jax.lax import all_to_all, axis_size
 
 E = 32
 K = 4
@@ -41,7 +42,9 @@
     my_pool = pools_all[lax.axis_index("dp")]
     my_coef = merge_coefficients(expert_ids, merge_weights, my_pool)
     member_table = (pools_all.T[:, :, None] == every_expert[None, None, :]).astype(jnp.bfloat16)
-    stripes = lax.all_to_all(down_table, "dp", split_axis=2, concat_axis=1, tiled=True)
+    stripes = jnp.concatenate(
+        all_to_all(jnp.stack(jnp.split(down_table, axis_size("dp"), axis=2)), "dp", 0, 0), axis=1
+    )
     by_expert = jnp.take(stripes, owner_slot, axis=1)
     outgoing = jnp.take(by_expert, pools_all.T, axis=1).reshape(ff_local, POOL, width)
     panel_set = lax.all_to_all(outgoing, "dp", split_axis=2, concat_axis=2, tiled=True)

time: 480 us -> 514 us (1.071)
  local copies, waits for them, and re-layouts: 72.6 us -> 112 us
  other arithmetic: 36.2 us -> 24.6 us
  blocking collectives: 140 us -> 147 us
    unnamed x20 -> x144, local copies, waits for them, and re-layouts: 17.2 us -> 51.7 us
    unnamed x1 -> x0, other arithmetic: 11.6 us -> none
    all_gather x1, blocking collectives: 50.6 us -> 57.6 us  [body(): lax.all_gather(expert_ids, 'dp', axis=0, tiled=True)]
  transfers between devices with their start and end apart: 5 -> 5, of which waited for: 2 -> 2; matrix products, arithmetic and copies ran while one was open for 11% -> 10% of each run, Pallas kernels for 0% -> 0%
where the time goes in v1:
time: 514 us; the launch traced here: 513 us
  waiting for transfers between devices  176 us (34%)
  blocking collectives  147 us (29%)
  local copies, waits for them, and re-layouts  112 us (22%)
  starting transfers between devices  30.1 us (6%)
  other arithmetic  24.6 us (5%)
  between operations  14.4 us (3%)
  matrix products  8.77 us (2%)
    all_to_all x1, waiting for transfers between devices, body(): lax.all_to_all(outgoing, 'dp', split_axis=2, concat_axis=2, tiled=True)  123 us
    all_gather x1, blocking collectives, body(): lax.all_gather(expert_ids, 'dp', axis=0, tiled=True)  57.6 us
    all_gather x1, blocking collectives, body(): lax.all_gather(merge_weights, 'dp', axis=0, tiled=True)  53.9 us
    all_gather x1, waiting for transfers between devices, body(): full_cot = lax.all_gather(cotangent, 'tensor', axis=1, tiled=True)  53 us
    unnamed x144, local copies, waits for them, and re-layouts  51.7 us
    all_to_all x1, blocking collectives, body(): lax.all_to_all(slotted.astype(jnp.bfloat16), 'dp', split_axis=1, concat_a...  35.5 us
    select_n x1, local copies, waits for them, and re-layouts, body(): jnp.take(by_expert, pools_all.T, axis=1).reshape(ff_local, POOL, width)  22.3 us
    gather x1, local copies, waits for them, and re-layouts, body(): jnp.take(by_expert, pools_all.T, axis=1).reshape(ff_local, POOL, width)  13.3 us
  transfers between devices with their start and end apart: 5, of which 2 were waited for; matrix products, arithmetic and copies ran while one was open for 10% of the time, Pallas kernels for 0%

profile of v1, /device:TPU:1, one launch (start us, length us, event | category | flops | bytes accessed | tf_op | source)
XLA Modules:
  0.0 512.8 jit_solution(2143279396814339660)
XLA Ops:
  7.2 1.2 fusion.21
  8.3 2.2 fusion.20
  11.1 0.6 constant_dynamic-update-slice_fusion.63
  12.3 0.9 copy.354
  13.1 0.9 copy.355
  18.8 0.6 constant_dynamic-update-slice_fusion.62
  19.4 0.6 constant_dynamic-update-slice_fusion.61
  20.0 0.6 constant_dynamic-update-slice_fusion.60
  21.8 0.6 constant_dynamic-update-slice_fusion.57
  22.5 0.6 constant_dynamic-update-slice_fusion.56
  23.1 0.6 constant_dynamic-update-slice_fusion.55
  23.7 0.6 constant_dynamic-update-slice_fusion.54
  24.3 0.6 constant_dynamic-update-slice_fusion.53
  24.9 0.6 constant_dynamic-update-slice_fusion.52
  25.5 0.6 constant_dynamic-update-slice_fusion.51
  27.3 0.6 constant_dynamic-update-slice_fusion.48
  27.9 0.6 constant_dynamic-update-slice_fusion.47
  28.5 0.6 constant_dynamic-update-slice_fusion.46
  29.1 0.6 constant_dynamic-update-slice_fusion.45
  29.7 0.6 constant_dynamic-update-slice_fusion.44
  57.0 11.6 %all-to-all-start = ((bf16[64,176,1,32]{1,3,2,0:T(8,128)(2,1)}), bf16[64,176,1,32]{1,3,2,0:T(8,128)(2,1)S(1)}, u32[]{:S(2)}, u32[]{:S(2)}) async-start(bf16[64,176,1,32]{1,3,2,0:T(8,128)(2,1)} %constant_dynamic-update-slice_fusion), calls=%async_computation | async-start | bytes 2097152 | tf_op jit(solution)/shard_map/all_to_all | solution.py:46
  68.7 57.6 %all-gather = s32[64,2,4]{2,1,0:T(2,128)S(1)} all-gather(s32[1,2,4]{2,1,0:T(2,128)S(1)} %bitcast.191), channel_id=1, replica_groups=mesh['dp'=64,'tensor'=8] {'dp'}, dimensions={0}, use_global_device_ids=true | all-gather | bytes 2080 | tf_op jit(solution)/shard_map/all_gather | solution.py:36
  128.1 13.3 %gather_fusion.1 = bf16[384,176,32]{1,2,0:T(8,128)(2,1)} fusion(bf16[176,32,32]{0,2,1:T(8,128)(2,1)S(1)} %select_bitcast_fusion, s32[1024]{0:T(1024)S(1)} %pad_clamp_fusion), kind=kCustom, calls=%fused_computation.1 | custom fusion | bytes 8652288 | tf_op jit(solution)/shard_map/jit(_take)/gather | solution.py:49
  141.4 6.2 %broadcast_select_fusion = bf16[176,6,2048]{0,2,1:T(8,128)(2,1)S(1)} fusion(bf16[176,6,2048]{0,2,1:T(8,128)(2,1)} %bitcast.179, pred[6,2048]{1,0:T(8,128)(4,1)S(1)} %broadcast_in_dim.86), kind=kLoop, calls=%fused_computation.7 | loop fusion | flops 2162688 | bytes 8663040 | tf_op jit(solution)/shard_map/jit(_take)/select_n | solution.py:49
  147.6 22.3 %copy.334 = bf16[176,6,2048]{0,1,2:T(8,128)(2,1)} copy(bf16[176,6,2048]{0,2,1:T(8,128)(2,1)S(1)} %broadcast_select_fusion) | data formatting | bytes 8650752 | tf_op jit(solution)/shard_map/jit(_take)/select_n | solution.py:49
  169.9 8.3 %all-to-all-start.1 = ((bf16[176,6,2048]{0,1,2:T(8,128)(2,1)}), bf16[176,6,2048]{0,1,2:T(8,128)(2,1)}, u32[]{:S(2)}, u32[]{:S(2)}) async-start(bf16[176,6,2048]{0,1,2:T(8,128)(2,1)} %copy.334), calls=%async_computation.1 | async-start | bytes 16777216 | tf_op jit(solution)/shard_map/all_to_all | solution.py:50
  178.3 0.7 all-gather.4.cloned.1.call-update
  179.0 53.0 %all-gather.4.cloned.1.call-done = bf16[512,2048]{1,0:T(8,128)(2,1)} async-done(((bf16[512,256]{1,0:T(8,128)(2,1)}), bf16[512,2048]{1,0:T(8,128)(2,1)}) %all-gather.4.cloned.1.call-update) | async-done | bytes 2097168 | tf_op jit(solution)/shard_map/all_gather | solution.py:61
  232.0 2.1 fusion.2
  234.1 3.8 copy.339
  237.9 122.7 %all-to-all-done.1 = bf16[176,6,2048]{0,1,2:T(8,128)(2,1)} async-done(((bf16[176,6,2048]{0,1,2:T(8,128)(2,1)}), bf16[176,6,2048]{0,1,2:T(8,128)(2,1)}, u32[]{:S(2)}, u32[]{:S(2)}) %all-to-all-start.1) | async-done | bytes 4325408 | tf_op jit(solution)/shard_map/all_to_all | solution.py:50
  360.6 10.1 %all-to-all-start.2 = ((bf16[176,2,2048]{0,1,2:T(2,128)(2,1)}), bf16[176,2,2048]{0,1,2:T(2,128)(2,1)S(1)}, u32[]{:S(2)}, u32[]{:S(2)}) async-start(bf16[176,2,2048]{0,1,2:T(2,128)(2,1)} %copy.339), calls=%async_computation.3 | async-start | bytes 4194304 | tf_op jit(solution)/shard_map/all_to_all | solution.py:71
  371.0 11.3 %copy.335 = bf16[176,6,2048]{2,0,1:T(8,128)(2,1)} copy(bf16[176,6,2048]{0,1,2:T(8,128)(2,1)} %all-to-all-done.1) | data formatting | bytes 8650752 | tf_op jit(solution)/shard_map/all_to_all | solution.py:50
  382.3 6.6 %convert_element_type.68 = f32[176,6,2048]{2,0,1:T(8,128)} convert(bf16[176,6,2048]{2,0,1:T(8,128)(2,1)} %copy.335) | non-fusion elementwise | flops 2162688 | bytes 12976128 | tf_op jit(solution)/shard_map/convert_element_type | solution.py:52
  388.9 4.8 multiply_reduce_fusion.1
  393.7 1.1 copy-done
  394.8 2.1 convolution_convert_fusion
  397.0 53.9 %all-gather.1 = f32[64,2,4]{2,1,0:T(2,128)S(1)} all-gather(f32[1,2,4]{2,1,0:T(2,128)S(1)} %bitcast.192), channel_id=1, replica_groups=mesh['dp'=64,'tensor'=8] {'dp'}, dimensions={0}, use_global_device_ids=true | all-gather | bytes 2080 | tf_op jit(solution)/shard_map/all_gather | solution.py:37
  451.0 0.6 bitcast_convert_fusion.1
  451.6 4.2 multiply_reduce_fusion
  455.8 3.7 fusion.3
  459.5 0.6 copy.344
  460.4 1.6 scatter_fusion
  462.1 35.5 %all_to_all.24 = bf16[176,64,32]{0,2,1:T(8,128)(2,1)S(1)} all-to-all(bf16[176,64,32]{0,2,1:T(8,128)(2,1)S(1)} %convert_element_type.80), channel_id=1, replica_groups=mesh['dp'=64,'tensor'=8] {'dp'}, dimensions={1} | all-to-all | bytes 1441792 | tf_op jit(solution)/shard_map/all_to_all | solution.py:87
  497.7 1.5 bitcast_convert_fusion
  499.1 5.3 %copy.345 = f32[176,1,2048]{2,1,0:T(1,128)} copy(f32[176,1,2048]{0,2,1:T(8,128)} %bitcast_convert_fusion) | data formatting | bytes 2883584
  504.4 0.8 fusion.6
  505.2 0.7 copy.412
  (158 shorter events, 37.4 us)
Async XLA Ops:
  7.2 3.4 copy-start.2
  16.6 52.1 %copy-start.5 = (s32[2,4]{1,0:T(2,128)S(1)}, s32[2,4]{1,0:T(2,128)}, u32[]{:S(2)}) copy-start(s32[2,4]{1,0:T(2,128)} %param.9) | copy-start | bytes 100
  17.3 110.0 %copy-start.7 = (s32[32]{0:T(128)S(1)}, s32[32]{0:T(128)}, u32[]{:S(2)}) copy-start(s32[32]{0:T(128)} %param.11) | copy-start | bytes 388
  57.0 70.3 %all-to-all-start = ((bf16[64,176,1,32]{1,3,2,0:T(8,128)(2,1)}), bf16[64,176,1,32]{1,3,2,0:T(8,128)(2,1)S(1)}, u32[]{:S(2)}, u32[]{:S(2)}) async-start(bf16[64,176,1,32]{1,3,2,0:T(8,128)(2,1)} %constant_dynamic-update-slice_fusion), calls=%async_computation | async-start | bytes 2097152 | tf_op jit(solution)/shard_map/all_to_all | solution.py:46
  169.9 62.0 %copy-start.4 = (bf16[512,176]{0,1:T(8,128)(2,1)S(1)}, bf16[512,176]{0,1:T(8,128)(2,1)}, u32[]{:S(2)}) copy-start(bf16[512,176]{0,1:T(8,128)(2,1)} %param.6) | copy-start | bytes 540676
  169.9 190.7 %all-to-all-start.1 = ((bf16[176,6,2048]{0,1,2:T(8,128)(2,1)}), bf16[176,6,2048]{0,1,2:T(8,128)(2,1)}, u32[]{:S(2)}, u32[]{:S(2)}) async-start(bf16[176,6,2048]{0,1,2:T(8,128)(2,1)} %copy.334), calls=%async_computation.1 | async-start | bytes 16777216 | tf_op jit(solution)/shard_map/all_to_all | solution.py:50
  178.3 53.7 %all-gather.4.cloned.1.call-start = ((), (), s32[]{:S(2)}) async-start(), calls=%async_computation.6 | async-start | bytes 2359296 | tf_op jit(solution)/shard_map/all_gather | solution.py:61
  237.9 133.0 %copy-start.6 = (f32[2,4]{1,0:T(2,128)S(1)}, f32[2,4]{1,0:T(2,128)}, u32[]{:S(2)}) copy-start(f32[2,4]{1,0:T(2,128)} %param.10) | copy-start | bytes 100
  360.6 90.3 %all-to-all-start.2 = ((bf16[176,2,2048]{0,1,2:T(2,128)(2,1)}), bf16[176,2,2048]{0,1,2:T(2,128)(2,1)S(1)}, u32[]{:S(2)}, u32[]{:S(2)}) async-start(bf16[176,2,2048]{0,1,2:T(2,128)(2,1)} %copy.339), calls=%async_computation.3 | async-start | bytes 4194304 | tf_op jit(solution)/shard_map/all_to_all | solution.py:71
  370.7 135.2 %reduce-scatter.2.cloned.1.call-start = ((), (), s32[]{:S(2)}) async-start(), calls=%async_computation.5 | async-start | bytes 2359296 | tf_op jit(solution)/shard_map/reduce_scatter | solution.py:58
  393.7 1.1 copy-start
  497.6 6.7 %copy-start.1 = (bf16[176,2,2048]{2,0,1:T(8,128)(2,1)S(1)}, bf16[176,2,2048]{2,0,1:T(8,128)(2,1)}, u32[]{:S(2)}) copy-start(bf16[176,2,2048]{2,0,1:T(8,128)(2,1)} %copy-done) | copy-start | bytes 4325380
  497.6 6.7 %copy-start.3 = (bf16[512,2048]{1,0:T(8,128)(2,1)S(1)}, bf16[512,2048]{1,0:T(8,128)(2,1)}, u32[]{:S(2)}) copy-start(bf16[512,2048]{1,0:T(8,128)(2,1)} %all-gather.4.cloned.1.call-done) | copy-start | bytes 6291460
Sparse Core Ops, SparseCore 0:
  181.1 50.8 all-gather.3
  397.1 45.3 reduce-scatter.1
